TPU v7x, 512 devices: a whole 4x4x16 slice. The times are simulated.
512 devices in a mesh: dp: 16 (over y, x), tensor: 32 (over z, core).
Axes of the slice: x: 4, y: 4, z: 16, core: 2. Of those that a mesh axis runs over, the one named last changes fastest.
Arguments:
- inputs: bfloat16 [2048, 4096], P('dp', 'tensor'), may hold values from -6 to 6
- cotangent: bfloat16 [2048, 4096], P('dp', 'tensor'), may hold values from -6 to 6
- gate_w: bfloat16 [32, 24, 128, 128], P('tensor'), may hold values from -0.25 to 0.25
- up_w: bfloat16 [32, 24, 128, 128], P('tensor'), may hold values from -0.25 to 0.25
- down_w: bfloat16 [32, 24, 128, 128], P('tensor'), may hold values from -0.25 to 0.25
- gate_list: int32 [32, 24], P('tensor'), may hold values from -1 to 127, as said below
- up_list: int32 [32, 24], P('tensor'), may hold values from -1 to 127, as said below
- down_list: int32 [32, 24], P('tensor'), may hold values from -1 to 127, as said below
Outputs:
- grad_x: bfloat16 [2048, 4096], P('dp', 'tensor')
- grad_gate_w: bfloat16 [32, 24, 128, 128], P('tensor', None, 'dp')
- grad_up_w: bfloat16 [32, 24, 128, 128], P('tensor', None, 'dp')
- grad_down_w: bfloat16 [32, 24, 128, 128], P('tensor', None, 'dp')
Inputs may be any that keep to these rules, and one draw needn't show every extreme that they name: `gate_list`: row j of the list names blocks of hidden blocks j * 4 to j * 4 + 3 only; no entry appears twice in a row; live entries come first and -1 fills the rest; a row holds at most 24 live entries and some row holds exactly 24. `up_list`: as for gate_list, drawn independently. `down_list`: as for gate_list, drawn independently.
All inputs are finite; a program needn't handle non-finite values.
Results may differ from a plain program's by a relative error of at most 0.014.
Values may be sent and summed in bfloat16 or wider, within the bound.
No kernel may reach another device: no remote copies, remote signals or barrier semaphores. Data moves between devices by JAX's collectives and lax.ppermute only.
A program may use at most 64 MiB of HBM per device.

v0:
```python
import math
import jax
import jax.numpy as jnp
from jax import lax
from jax.sharding import PartitionSpec as P

D = 4096
FF = 16384
BLOCK = 128


def decode(entries, row_count):
    living = entries >= 0
    clamped = jnp.maximum(entries, 0)
    return (living, clamped // row_count, clamped % row_count)


def one_hot(block_index, width_count, living):
    return ((block_index[:, None] == jnp.arange(width_count)[None, :]) & living[:, None]).astype(
        jnp.float32
    )


def select_sum(values, table):
    return jnp.sum(values[:, :, None, :] * table[None, :, :, None], axis=1)


def project_rows(blocks_in, weights, rows_hot):
    products = jnp.einsum("tkc,kch->tkh", blocks_in, weights, preferred_element_type=jnp.float32)
    return select_sum(products, rows_hot)


def weight_term(products, grad_scale, living):
    rounded = (products * grad_scale).astype(jnp.bfloat16)
    rounded = lax.optimization_barrier(rounded)
    return (rounded.astype(jnp.float32) * living[:, None, None].astype(jnp.float32))[None]


def add_sources(received):
    return jnp.sum(received.astype(jnp.float32), axis=1)


def on_device(inputs, cotangent, gate_w, up_w, down_w, gate_list, up_list, down_list):
    tensor_size = lax.axis_size("tensor")
    hidden_rows = FF // (BLOCK * tensor_size)
    feat_blocks = D // BLOCK
    tokens_here = inputs.shape[0]
    grad_scale = 1.0 / math.sqrt(tokens_here * lax.axis_size("dp"))
    gate_live, gate_feat, gate_row = decode(gate_list[0], hidden_rows)
    up_live, up_feat, up_row = decode(up_list[0], hidden_rows)
    down_live, down_feat, down_row = decode(down_list[0], hidden_rows)
    whole_in, whole_cot = (
        lax.all_gather(inputs, "tensor", axis=1, tiled=True),
        lax.all_gather(cotangent, "tensor", axis=1, tiled=True),
    )
    input_blocks = whole_in.reshape(tokens_here, feat_blocks, BLOCK)
    gate_in = jnp.take(input_blocks, gate_feat, axis=1)
    up_in = jnp.take(input_blocks, up_feat, axis=1)
    gate_val = project_rows(gate_in, gate_w[0], one_hot(gate_row, hidden_rows, gate_live))
    up_val = project_rows(up_in, up_w[0], one_hot(up_row, hidden_rows, up_live))
    sigmoid_gate = jax.nn.sigmoid(gate_val)
    active = gate_val * sigmoid_gate
    hidden = (active * up_val).astype(jnp.bfloat16)
    cot_blocks = whole_cot.reshape(tokens_here, feat_blocks, BLOCK)
    down_cot = jnp.take(cot_blocks, down_feat, axis=1)
    hidden_down = jnp.take(hidden, down_row, axis=1)
    down_part = jnp.einsum("tkc,khc->tkh", down_cot, down_w[0], preferred_element_type=jnp.float32)
    grad_hidden = select_sum(down_part, one_hot(down_row, hidden_rows, down_live))
    down_term = weight_term(
        jnp.einsum("tkh,tkc->khc", hidden_down, down_cot, preferred_element_type=jnp.float32),
        grad_scale,
        down_live,
    )
    grad_gate = (
        grad_hidden * up_val * sigmoid_gate * (1.0 + gate_val * (1.0 - sigmoid_gate))
    ).astype(jnp.bfloat16)
    grad_up = (grad_hidden * active).astype(jnp.bfloat16)
    gate_back = jnp.take(grad_gate, gate_row, axis=1)
    up_back = jnp.take(grad_up, up_row, axis=1)
    gate_term = weight_term(
        jnp.einsum("tkc,tkh->kch", gate_in, gate_back, preferred_element_type=jnp.float32),
        grad_scale,
        gate_live,
    )
    up_term = weight_term(
        jnp.einsum("tkc,tkh->kch", up_in, up_back, preferred_element_type=jnp.float32),
        grad_scale,
        up_live,
    )
    back_gate = jnp.einsum("tkh,kch->tkc", gate_back, gate_w[0], preferred_element_type=jnp.float32)
    back_up = jnp.einsum("tkh,kch->tkc", up_back, up_w[0], preferred_element_type=jnp.float32)
    partial_sum = select_sum(back_gate, one_hot(gate_feat, feat_blocks, gate_live))
    partial_sum = partial_sum + select_sum(back_up, one_hot(up_feat, feat_blocks, up_live))
    pieces = partial_sum.astype(jnp.bfloat16)
    summed = add_sources(lax.all_to_all(pieces, "tensor", split_axis=1, concat_axis=1, tiled=True))
    grad_x = summed.astype(jnp.bfloat16)
    gate_sum, up_sum, down_sum = (
        lax.psum_scatter(
            gate_term.astype(jnp.bfloat16), "dp", scatter_dimension=2, tiled=True
        ).astype(jnp.float32),
        lax.psum_scatter(
            up_term.astype(jnp.bfloat16), "dp", scatter_dimension=2, tiled=True
        ).astype(jnp.float32),
        lax.psum_scatter(
            down_term.astype(jnp.bfloat16), "dp", scatter_dimension=2, tiled=True
        ).astype(jnp.float32),
    )
    return (
        grad_x,
        gate_sum.astype(jnp.bfloat16),
        up_sum.astype(jnp.bfloat16),
        down_sum.astype(jnp.bfloat16),
    )


def solution(mesh):
    return jax.shard_map(
        on_device,
        mesh=mesh,
        in_specs=(
            P("dp", "tensor"),
            P("dp", "tensor"),
            P("tensor", None, None, None),
            P("tensor", None, None, None),
            P("tensor", None, None, None),
            P("tensor", None),
            P("tensor", None),
            P("tensor", None),
        ),
        out_specs=(
            P("dp", "tensor"),
            P("tensor", None, "dp", None),
            P("tensor", None, "dp", None),
            P("tensor", None, "dp", None),
        ),
        check_vma=False,
    )
```

profile of v0, /device:TPU:32, one launch (start us, length us, event | category | flops | bytes accessed | tf_op | source)
XLA Modules:
  0.0 357.0 jit_solution(7031194713557921426)
XLA Ops:
  7.2 0.0 copy-start
  7.2 0.0 all-gather.5.cloned.1.call-start
  7.2 1.5 copy.56
  8.8 0.0 all-gather.5.cloned.1.call-update
  8.8 0.0 all-gather.3.cloned.1.call-start
  8.8 1.5 copy.53
  10.3 0.0 all-gather.3.cloned.1.call-update
  10.3 0.7 compare_and_fusion.4
  11.0 1.2 fusion.45
  12.3 1.2 compare_and_fusion.2
  13.5 1.2 fusion.46
  14.8 1.2 compare_and_fusion.5
  16.0 0.6 pad_clamp_fusion.2
  16.6 1.2 fusion.44
  17.8 0.1 fusion.26
  17.9 0.7 fusion.24
  18.6 66.7 %all-gather.5.cloned.1.call-done = bf16[128,4096]{0,1:T(8,128)(2,1)} async-done(((bf16[128,128]{0,1:T(8,128)(2,1)}), bf16[128,4096]{0,1:T(8,128)(2,1)}) %all-gather.5.cloned.1.call-update) | async-done | bytes 1048592 | tf_op jit(solution)/shard_map/all_gather | solution.py:53
  85.2 1.6 copy.57
  86.9 0.7 gather_fusion.1
  87.6 0.9 copy-done.2
  88.5 0.4 convolution_bitcast_fusion.3
  88.9 0.9 copy.58
  89.8 1.6 gather_fusion.2
  91.4 1.8 convolution_bitcast_fusion.2
  93.2 2.1 copy.62
  95.2 60.6 %all-gather.3.cloned.1.call-done = bf16[128,4096]{0,1:T(8,128)(2,1)} async-done(((bf16[128,128]{0,1:T(8,128)(2,1)}), bf16[128,4096]{0,1:T(8,128)(2,1)}) %all-gather.3.cloned.1.call-update) | async-done | bytes 1048592 | tf_op jit(solution)/shard_map/all_gather | solution.py:54
  155.8 1.8 copy.54
  157.6 1.6 gather_fusion
  159.2 2.1 convolution_bitcast_fusion.4
  161.3 0.9 copy.55
  162.2 1.8 multiply_reduce_fusion.4
  164.0 3.5 multiply_reduce_fusion.2
  167.5 0.2 multiply_convert_fusion.6
  167.7 0.7 gather_fusion.4
  168.4 0.7 convolution_bitcast_fusion
  169.1 0.2 copy-done.6
  169.3 0.9 copy.68
  170.2 0.8 gather_fusion.3
  171.0 2.1 convolution_bitcast_fusion.1
  173.2 0.9 copy.65
  174.1 0.0 copy-start.11
  174.1 13.1 %multiply_reduce_fusion = f32[128,32,128]{2,1,0:T(8,128)S(1)} fusion(f32[24,32]{1,0:T(8,128)S(1)} %fusion.26, f32[128,24,128]{2,1,0:T(8,128)S(1)} %copy.68), kind=kLoop, calls=%fused_computation.6 | loop fusion | flops 24641536 | bytes 3673088 | tf_op jit(solution)/shard_map/reduce_sum | solution.py:25
  187.2 13.3 %multiply_reduce_fusion.1 = f32[128,32,128]{2,1,0:T(8,128)S(1)} fusion(f32[24,32]{1,0:T(8,128)S(1)} %copy-done.11, f32[128,24,128]{2,1,0:T(8,128)S(1)} %copy.65), kind=kLoop, calls=%fused_computation.7 | loop fusion | flops 24641536 | bytes 3673088 | tf_op jit(solution)/shard_map/reduce_sum | solution.py:25
  200.6 0.5 add_convert_fusion
  201.1 1.4 copy.69
  202.5 9.0 %all-to-all-start = ((bf16[128,32,128]{2,0,1:T(8,128)(2,1)}), bf16[128,32,128]{2,0,1:T(8,128)(2,1)S(1)}, u32[]{:S(2)}, u32[]{:S(2)}) async-start(bf16[128,32,128]{2,0,1:T(8,128)(2,1)} %copy.69), calls=%async_computation | async-start | bytes 2097152 | tf_op jit(solution)/shard_map/all_to_all | solution.py:95
  211.5 0.0 all-reduce.6.cloned.1.call-start
  211.6 2.6 multiply_convert_fusion.3
  214.3 1.4 multiply_convert_fusion.5
  215.7 0.7 gather_fusion.5
  216.4 0.4 copy-done.5
  216.8 0.5 multiply_convert_fusion.1
  217.4 0.6 copy-done.9
  218.0 1.1 fusion.1
  219.1 1.1 fusion
  220.2 1.1 fusion.2
  221.3 0.0 all-reduce.6.cloned.1.call-update
  221.4 1.3 dynamic-slice
  223.3 122.1 %all-reduce.6.cloned.1.call-done = (bf16[1,24,128,128]{3,2,1,0:T(8,128)(2,1)}, bf16[1,24,128,128]{3,2,1,0:T(8,128)(2,1)}, bf16[1,24,128,128]{3,2,1,0:T(8,128)(2,1)}) async-done(((bf16[1,24,128,128]{3,2,1,0:T(8,128)(2,1)}, bf16[1,24,128,128]{3,2,1,0:T(8,128)(2,1)}, bf16[1,24,128,128]{3,2,1,0:T(8,128)(2,1)}), (bf16[1,24,128,128]{3,2,1,0:T(8,128)(2,1)}, bf16[1,24,128,128]{3,2,1,0:T(8,128)(2,1)}, ...) | async-done | bytes 2359312
  345.4 1.4 constant_dynamic-slice_fusion
  346.9 1.4 constant_dynamic-slice_fusion.1
  348.3 1.4 constant_dynamic-slice_fusion.2
  349.7 0.0 all-to-all-done
  349.7 0.8 reduce_sum.62
  (59 shorter events, 0.2 us)
Async XLA Ops:
  7.2 81.3 %copy-start = (bf16[1,24,128,128]{3,2,1,0:T(8,128)(2,1)S(1)}, bf16[1,24,128,128]{3,2,1,0:T(8,128)(2,1)}, u32[]{:S(2)}) copy-start(bf16[1,24,128,128]{3,2,1,0:T(8,128)(2,1)} %param.15) | copy-start | bytes 2359300
  7.2 78.1 %all-gather.5.cloned.1.call-start = ((), (), s32[]{:S(2)}) async-start(), calls=%async_computation.2 | async-start | bytes 1081344 | tf_op jit(solution)/shard_map/all_gather | solution.py:53
  8.8 147.0 %all-gather.3.cloned.1.call-start = ((), (), s32[]{:S(2)}) async-start(), calls=%async_computation.1 | async-start | bytes 1081344 | tf_op jit(solution)/shard_map/all_gather | solution.py:54
  11.0 76.6 %copy-start.12 = (pred[24]{0:T(512)(128)(4,1)}, pred[24]{0:T(512)(128)(4,1)S(1)}, u32[]{:S(2)}) copy-start(pred[24]{0:T(512)(128)(4,1)S(1)} %get-tuple-element.17) | copy-start | bytes 76
  11.0 157.4 %copy-start.14 = (pred[24]{0:T(512)(128)(4,1)}, pred[24]{0:T(512)(128)(4,1)S(1)}, u32[]{:S(2)}) copy-start(pred[24]{0:T(512)(128)(4,1)S(1)} %get-tuple-element.32) | copy-start | bytes 76
  13.5 77.9 %copy-start.18 = (pred[24]{0:T(512)(128)(4,1)}, pred[24]{0:T(512)(128)(4,1)S(1)}, u32[]{:S(2)}) copy-start(pred[24]{0:T(512)(128)(4,1)S(1)} %get-tuple-element.34) | copy-start | bytes 76
  16.0 143.2 %copy-start.20 = (pred[24]{0:T(512)(128)(4,1)}, pred[24]{0:T(512)(128)(4,1)S(1)}, u32[]{:S(2)}) copy-start(pred[24]{0:T(512)(128)(4,1)S(1)} %get-tuple-element.15) | copy-start | bytes 76
  87.6 0.9 copy-start.2
  162.2 1.8 copy-start.1
  168.4 0.9 copy-start.6
  170.2 0.9 copy-start.16
  171.0 2.1 copy-start.7
  174.1 13.1 %copy-start.11 = (f32[24,32]{1,0:T(8,128)S(1)}, f32[24,32]{1,0:T(8,128)}, u32[]{:S(2)}) copy-start(f32[24,32]{1,0:T(8,128)} %fusion.24) | copy-start | bytes 9220
  202.5 9.1 %copy-start.3 = (bf16[24,128,128]{2,1,0:T(8,128)(2,1)S(1)}, bf16[24,128,128]{2,1,0:T(8,128)(2,1)}, u32[]{:S(2)}) copy-start(bf16[24,128,128]{2,1,0:T(8,128)(2,1)} %copy-done.2) | copy-start | bytes 2359300
  202.5 9.1 %copy-start.13 = (pred[24]{0:T(512)(128)(4,1)S(1)}, pred[24]{0:T(512)(128)(4,1)}, u32[]{:S(2)}) copy-start(pred[24]{0:T(512)(128)(4,1)} %copy-done.12) | copy-start | bytes 76
  202.5 9.1 %copy-start.15 = (pred[24]{0:T(512)(128)(4,1)S(1)}, pred[24]{0:T(512)(128)(4,1)}, u32[]{:S(2)}) copy-start(pred[24]{0:T(512)(128)(4,1)} %copy-done.14) | copy-start | bytes 76
  202.5 147.2 %all-to-all-start = ((bf16[128,32,128]{2,0,1:T(8,128)(2,1)}), bf16[128,32,128]{2,0,1:T(8,128)(2,1)S(1)}, u32[]{:S(2)}, u32[]{:S(2)}) async-start(bf16[128,32,128]{2,0,1:T(8,128)(2,1)} %copy.69), calls=%async_computation | async-start | bytes 2097152 | tf_op jit(solution)/shard_map/all_to_all | solution.py:95
  211.5 2.7 copy-start.4
  211.5 2.7 copy-start.17
  211.5 133.9 %all-reduce.6.cloned.1.call-start = ((), (), s32[]{:S(2)}) async-start(), calls=%async_computation.3 | async-start | bytes 4718592
  211.6 2.7 copy-start.8
  211.6 2.6 copy-start.19
  215.7 1.1 copy-start.5
  215.7 1.1 copy-start.21
  215.7 1.1 copy-start.25
  216.8 1.1 copy-start.9
  216.8 1.1 copy-start.22
  217.4 1.7 copy-start.10
  217.4 1.7 copy-start.23
  218.0 2.2 copy-start.24
Sparse Core Ops, SparseCore 0:
  10.7 74.5 all-gather.4
  87.9 67.8 all-gather.2
  221.5 123.9 all-reduce.5
where the time goes:
time: 358 us; the launch traced here: 357 us
  waiting for transfers between devices  249 us (70%)
  other arithmetic  44.7 us (12%)
  local copies, waits for them, and re-layouts  27.3 us (8%)
  between operations  14.8 us (4%)
  matrix products  11.6 us (3%)
  starting transfers between devices  9.13 us (3%)
    unnamed x4, waiting for transfers between devices  122 us
    all_gather x1, waiting for transfers between devices, on_device(): lax.all_gather(inputs, 'tensor', axis=1, tiled=True)  66.7 us
    all_gather x1, waiting for transfers between devices, on_device(): lax.all_gather(cotangent, 'tensor', axis=1, tiled=True)  60.6 us
    reduce_sum x4, other arithmetic, select_sum(): return jnp.sum(values[:, :, None, :] * table[None, :, :, None], axis=1)  31.7 us
    unnamed x58, local copies, waits for them, and re-layouts  10.7 us
    all_to_all x1, starting transfers between devices, on_device(): lax.all_to_all(pieces, 'tensor', split_axis=1, concat_axis=1, tiled=True)  9 us
  transfers between devices with their start and end apart: 4, of which 3 were waited for; matrix products, arithmetic and copies ran while one was open for 9% of the time, Pallas kernels for 0%

commit v1 on v0

--- a/solution.py
+++ b/solution.py
@@ -1,3 +1,4 @@
+import functools
 import math
 import jax
 import jax.numpy as jnp
@@ -7,6 +8,18 @@
 D = 4096
 FF = 16384
 BLOCK = 128
+
+
+def produce_the_lines(incoming_x, which_axis, d0):
+    return jnp.concatenate(
+        lax.all_to_all(
+            jnp.stack(lax.axis_size(which_axis) * [incoming_x], axis=0), which_axis, 0, 0
+        ),
+        axis=d0,
+    )
+
+
+extend_ticks_by_axis = functools.partial(produce_the_lines, which_axis="tensor", d0=1)
 
 
 def decode(entries, row_count):
@@ -51,7 +64,7 @@
     down_live, down_feat, down_row = decode(down_list[0], hidden_rows)
     whole_in, whole_cot = (
         lax.all_gather(inputs, "tensor", axis=1, tiled=True),
-        lax.all_gather(cotangent, "tensor", axis=1, tiled=True),
+        extend_ticks_by_axis(cotangent),
     )
     input_blocks = whole_in.reshape(tokens_here, feat_blocks, BLOCK)
     gate_in = jnp.take(input_blocks, gate_feat, axis=1)

time: 358 us -> 302 us (0.84)
  waiting for transfers between devices: 249 us -> 185 us
  starting transfers between devices: 9.13 us -> 24.5 us
  other arithmetic: 44.7 us -> 40.4 us
    all_gather x1 -> x0, waiting for transfers between devices: 60.6 us -> none  [on_device(): lax.all_gather(cotangent, 'tensor', axis=1, tiled=True)]
    all_to_all x0 -> x1, starting transfers between devices: none -> 15.4 us  [produce_the_lines(): lax.all_to_all(jnp.stack(lax.axis_size(which_axis) * [incoming_x], axis=0...]
    unnamed x58 -> x65, local copies, waits for them, and re-layouts: 10.7 us -> 9.42 us
    unnamed x4 -> x3, waiting for transfers between devices: 122 us -> 122 us
  transfers between devices with their start and end apart: 4 -> 4, of which waited for: 3 -> 2; matrix products, arithmetic and copies ran while one was open for 9% -> 10% of each run, Pallas kernels for 0% -> 0%
where the time goes in v1:
time: 302 us
  waiting for transfers between devices  185 us (61%)
  other arithmetic  40.4 us (13%)
  local copies, waits for them, and re-layouts  25.7 us (9%)
  starting transfers between devices  24.5 us (8%)
  between operations  15.2 us (5%)
  matrix products  10.3 us (3%)
    unnamed x3, waiting for transfers between devices  122 us
    all_gather x1, waiting for transfers between devices, on_device(): lax.all_gather(inputs, 'tensor', axis=1, tiled=True)  63.1 us
    reduce_sum x4, other arithmetic, select_sum(): return jnp.sum(values[:, :, None, :] * table[None, :, :, None], axis=1)  31.5 us
    all_to_all x1, starting transfers between devices, produce_the_lines(): lax.all_to_all(jnp.stack(lax.axis_size(which_axis) * [incoming_x], axis=0...  15.4 us
    unnamed x65, local copies, waits for them, and re-layouts  9.42 us
    all_to_all x1, starting transfers between devices, on_device(): lax.all_to_all(pieces, 'tensor', split_axis=1, concat_axis=1, tiled=True)  9.03 us
  transfers between devices with their start and end apart: 4, of which 2 were waited for; matrix products, arithmetic and copies ran while one was open for 10% of the time, Pallas kernels for 0%

profile of v1, /device:TPU:32, one launch (start us, length us, event | category | flops | bytes accessed | tf_op | source)
XLA Modules:
  0.0 301.7 jit_solution(7538096695130679157)
XLA Ops:
  7.2 0.0 copy-start
  7.2 0.0 all-gather.2.cloned.1.call-start
  7.2 1.5 copy.50
  8.8 0.0 all-gather.2.cloned.1.call-update
  8.8 0.0 copy-start.26
  8.8 0.0 copy-start.27
  8.8 0.0 copy-start.28
  8.8 2.0 stack.2
  10.8 15.4 %all-to-all-start = ((bf16[32,128,128]{2,1,0:T(8,128)(2,1)}), bf16[32,128,128]{2,1,0:T(8,128)(2,1)}, u32[]{:S(2)}, u32[]{:S(2)}) async-start(bf16[32,128,128]{2,1,0:T(8,128)(2,1)} %stack.2), calls=%async_computation | async-start | bytes 2097152 | tf_op jit(solution)/shard_map/all_to_all | solution.py:15
  26.3 0.5 compare_and_fusion.2
  26.8 0.5 compare_and_fusion.5
  27.4 0.6 pad_clamp_fusion.2
  28.0 0.6 fusion.45
  28.6 0.5 fusion.46
  29.2 0.5 fusion.44
  29.7 0.1 fusion.26
  29.8 0.7 fusion.24
  30.5 63.1 %all-gather.2.cloned.1.call-done = bf16[128,4096]{0,1:T(8,128)(2,1)} async-done(((bf16[128,128]{0,1:T(8,128)(2,1)}), bf16[128,4096]{0,1:T(8,128)(2,1)}) %all-gather.2.cloned.1.call-update) | async-done | bytes 1048592 | tf_op jit(solution)/shard_map/all_gather | solution.py:66
  93.5 1.6 copy.51
  95.2 0.7 gather_fusion.1
  95.9 0.9 copy-done.1
  96.8 0.4 convolution_bitcast_fusion.3
  97.2 0.9 copy.52
  98.1 1.6 gather_fusion.2
  99.7 1.8 convolution_bitcast_fusion.2
  101.5 0.9 copy.56
  102.4 3.5 %multiply_reduce_fusion.2 = (f32[128,4,128]{2,1,0:T(4,128)S(1)}, f32[128,4,128]{2,1,0:T(4,128)S(1)}) fusion(f32[24,4]{0,1:T(4,128)S(1)} %fusion.32, f32[128,24,128]{2,1,0:T(8,128)S(1)} %copy.56, f32[24,4]{0,1:T(4,128)S(1)} %fusion.30, f32[128,24,128]{2,1,0:T(8,128)S(1)} %copy.52), kind=kLoop, calls=%fused_computation.8 | loop fusion | flops 6160384 | bytes 3670784 | tf_op jit(solution)/shard_map/reduce_sum | solution.py:38
  105.9 2.0 gather_fusion
  108.0 0.7 convolution_bitcast_fusion.4
  108.7 0.1 copy-done.4
  108.8 0.9 copy.49
  109.7 1.8 multiply_reduce_fusion.4
  111.5 0.2 multiply_convert_fusion.6
  111.7 0.7 gather_fusion.4
  112.4 0.7 convolution_bitcast_fusion
  113.1 0.2 copy-done.6
  113.3 0.9 copy.62
  114.2 0.0 copy-start.19
  114.2 1.0 gather_fusion.3
  115.2 2.1 convolution_bitcast_fusion.1
  117.3 1.1 copy.59
  118.4 0.0 copy-start.12
  118.5 13.1 %multiply_reduce_fusion = f32[128,32,128]{2,1,0:T(8,128)S(1)} fusion(f32[24,32]{1,0:T(8,128)S(1)} %fusion.26, f32[128,24,128]{2,1,0:T(8,128)S(1)} %copy.62), kind=kLoop, calls=%fused_computation.6 | loop fusion | flops 24641536 | bytes 3673088 | tf_op jit(solution)/shard_map/reduce_sum | solution.py:38
  131.6 13.1 %multiply_reduce_fusion.1 = f32[128,32,128]{2,1,0:T(8,128)S(1)} fusion(f32[24,32]{1,0:T(8,128)S(1)} %copy-done.12, f32[128,24,128]{2,1,0:T(8,128)S(1)} %copy.59), kind=kLoop, calls=%fused_computation.7 | loop fusion | flops 24641536 | bytes 3673088 | tf_op jit(solution)/shard_map/reduce_sum | solution.py:38
  144.7 0.5 add_convert_fusion
  145.2 1.4 copy.63
  146.6 9.0 %all-to-all-start.1 = ((bf16[128,32,128]{2,0,1:T(8,128)(2,1)}), bf16[128,32,128]{2,0,1:T(8,128)(2,1)S(1)}, u32[]{:S(2)}, u32[]{:S(2)}) async-start(bf16[128,32,128]{2,0,1:T(8,128)(2,1)} %copy.63), calls=%async_computation.1 | async-start | bytes 2097152 | tf_op jit(solution)/shard_map/all_to_all | solution.py:108
  155.7 0.0 all-reduce.6.cloned.1.call-start
  155.8 2.7 multiply_convert_fusion.3
  158.4 1.4 multiply_convert_fusion.5
  159.9 0.7 gather_fusion.5
  160.6 0.4 copy-done.5
  161.0 0.5 multiply_convert_fusion.1
  161.5 0.6 copy-done.9
  162.1 1.1 fusion.1
  163.2 1.1 fusion
  164.4 1.1 fusion.2
  165.5 0.0 all-reduce.6.cloned.1.call-update
  165.5 1.3 dynamic-slice
  167.5 122.4 %all-reduce.6.cloned.1.call-done = (bf16[1,24,128,128]{3,2,1,0:T(8,128)(2,1)}, bf16[1,24,128,128]{3,2,1,0:T(8,128)(2,1)}, bf16[1,24,128,128]{3,2,1,0:T(8,128)(2,1)}) async-done(((bf16[1,24,128,128]{3,2,1,0:T(8,128)(2,1)}, bf16[1,24,128,128]{3,2,1,0:T(8,128)(2,1)}, bf16[1,24,128,128]{3,2,1,0:T(8,128)(2,1)}), (bf16[1,24,128,128]{3,2,1,0:T(8,128)(2,1)}, bf16[1,24,128,128]{3,2,1,0:T(8,128)(2,1)}, ...) | async-done | bytes 2359312
  289.8 1.4 constant_dynamic-slice_fusion
  291.2 1.4 constant_dynamic-slice_fusion.1
  292.7 1.4 constant_dynamic-slice_fusion.2
  294.1 0.8 reduce_sum.62
  (65 shorter events, 0.2 us)
Async XLA Ops:
  7.2 89.6 %copy-start = (bf16[1,24,128,128]{3,2,1,0:T(8,128)(2,1)S(1)}, bf16[1,24,128,128]{3,2,1,0:T(8,128)(2,1)}, u32[]{:S(2)}) copy-start(bf16[1,24,128,128]{3,2,1,0:T(8,128)(2,1)} %param.15) | copy-start | bytes 2359300
  7.2 86.4 %all-gather.2.cloned.1.call-start = ((), (), s32[]{:S(2)}) async-start(), calls=%async_computation.2 | async-start | bytes 1081344 | tf_op jit(solution)/shard_map/all_gather | solution.py:66
  8.8 17.4 %copy-start.26 = (s32[1,24]{1,0:T(1,128)S(1)}, s32[1,24]{1,0:T(1,128)}, u32[]{:S(2)}) copy-start(s32[1,24]{1,0:T(1,128)} %param.18) | copy-start | bytes 292
  8.8 17.5 %copy-start.27 = (s32[1,24]{1,0:T(1,128)S(1)}, s32[1,24]{1,0:T(1,128)}, u32[]{:S(2)}) copy-start(s32[1,24]{1,0:T(1,128)} %param.17) | copy-start | bytes 292
  8.8 18.0 %copy-start.28 = (s32[1,24]{1,0:T(1,128)S(1)}, s32[1,24]{1,0:T(1,128)}, u32[]{:S(2)}) copy-start(s32[1,24]{1,0:T(1,128)} %param.19) | copy-start | bytes 292
  10.8 95.1 %all-to-all-start = ((bf16[32,128,128]{2,1,0:T(8,128)(2,1)}), bf16[32,128,128]{2,1,0:T(8,128)(2,1)}, u32[]{:S(2)}, u32[]{:S(2)}) async-start(bf16[32,128,128]{2,1,0:T(8,128)(2,1)} %stack.2), calls=%async_computation | async-start | bytes 2097152 | tf_op jit(solution)/shard_map/all_to_all | solution.py:15
  26.2 69.6 %copy-start.13 = (pred[24]{0:T(512)(128)(4,1)}, pred[24]{0:T(512)(128)(4,1)S(1)}, u32[]{:S(2)}) copy-start(pred[24]{0:T(512)(128)(4,1)S(1)} %get-tuple-element.17) | copy-start | bytes 76
  26.2 86.2 %copy-start.15 = (pred[24]{0:T(512)(128)(4,1)}, pred[24]{0:T(512)(128)(4,1)S(1)}, u32[]{:S(2)}) copy-start(pred[24]{0:T(512)(128)(4,1)S(1)} %get-tuple-element.32) | copy-start | bytes 76
  26.8 72.9 %copy-start.21 = (pred[24]{0:T(512)(128)(4,1)}, pred[24]{0:T(512)(128)(4,1)S(1)}, u32[]{:S(2)}) copy-start(pred[24]{0:T(512)(128)(4,1)S(1)} %get-tuple-element.34) | copy-start | bytes 76
  27.4 80.6 %copy-start.17 = (pred[24]{0:T(512)(128)(4,1)}, pred[24]{0:T(512)(128)(4,1)S(1)}, u32[]{:S(2)}) copy-start(pred[24]{0:T(512)(128)(4,1)S(1)} %get-tuple-element.15) | copy-start | bytes 76
  95.9 0.9 copy-start.1
  105.9 2.0 copy-start.11
  107.9 0.9 copy-start.4
  112.4 0.9 copy-start.6
  114.2 1.0 copy-start.19
  115.2 2.1 copy-start.7
  118.4 13.1 %copy-start.12 = (f32[24,32]{1,0:T(8,128)S(1)}, f32[24,32]{1,0:T(8,128)}, u32[]{:S(2)}) copy-start(f32[24,32]{1,0:T(8,128)} %fusion.24) | copy-start | bytes 9220
  146.6 9.1 %copy-start.2 = (bf16[24,128,128]{2,1,0:T(8,128)(2,1)S(1)}, bf16[24,128,128]{2,1,0:T(8,128)(2,1)}, u32[]{:S(2)}) copy-start(bf16[24,128,128]{2,1,0:T(8,128)(2,1)} %copy-done.1) | copy-start | bytes 2359300
  146.6 9.1 %copy-start.14 = (pred[24]{0:T(512)(128)(4,1)S(1)}, pred[24]{0:T(512)(128)(4,1)}, u32[]{:S(2)}) copy-start(pred[24]{0:T(512)(128)(4,1)} %copy-done.13) | copy-start | bytes 76
  146.6 9.1 %copy-start.16 = (pred[24]{0:T(512)(128)(4,1)S(1)}, pred[24]{0:T(512)(128)(4,1)}, u32[]{:S(2)}) copy-start(pred[24]{0:T(512)(128)(4,1)} %copy-done.15) | copy-start | bytes 76
  146.6 147.5 %all-to-all-start.1 = ((bf16[128,32,128]{2,0,1:T(8,128)(2,1)}), bf16[128,32,128]{2,0,1:T(8,128)(2,1)S(1)}, u32[]{:S(2)}, u32[]{:S(2)}) async-start(bf16[128,32,128]{2,0,1:T(8,128)(2,1)} %copy.63), calls=%async_computation.1 | async-start | bytes 2097152 | tf_op jit(solution)/shard_map/all_to_all | solution.py:108
  155.6 2.8 copy-start.3
  155.7 2.8 copy-start.20
  155.7 134.1 %all-reduce.6.cloned.1.call-start = ((), (), s32[]{:S(2)}) async-start(), calls=%async_computation.3 | async-start | bytes 4718592
  155.7 2.7 copy-start.8
  155.8 2.7 copy-start.22
  159.8 1.1 copy-start.5
  159.9 1.1 copy-start.18
  159.9 1.1 copy-start.29
  161.0 1.1 copy-start.9
  161.0 1.1 copy-start.25
  161.5 1.7 copy-start.10
  161.5 1.7 copy-start.24
  162.1 2.2 copy-start.23
Sparse Core Ops, SparseCore 0:
  10.7 82.8 all-gather.1
  165.6 124.1 all-reduce.5
